TPU v7x, 32 devices: a whole 2x2x4 slice. The times are simulated.
32 devices in a mesh: grp: 2 (over x), orient: 16 (over z, y, core).
Axes of the slice: x: 2, y: 2, z: 4, core: 2. Of those that a mesh axis runs over, the one named last changes fastest.
Arguments:
- particles: bfloat16 [2048, 2048], P(('grp', 'orient')), parts along dimension 0, may hold values from -50 to 50
- references: bfloat16 [4096, 2048], P(('grp', 'orient')), parts along dimension 0, may hold values from -4 to 4
- tile_blocks: int32 [32, 6], P('grp'), parts along dimension 0, may hold values from 0 to 7, as said below
- tile_count: int32 [32], P('grp'), parts along dimension 0, may hold values from 1 to 6
- shift_start: int32 [32, 6], P('grp'), parts along dimension 0, may hold values from 1 to 16
Outputs:
- ref_update: float32 [4096, 2048], P(('grp', 'orient')), parts along dimension 0
- weight_sum: float32 [4096], P(('grp', 'orient')), parts along dimension 0
- log_evidence: float32 [2048], P(('grp', 'orient')), parts along dimension 0
There are 2 independent parts, one for each index of `grp`. A program takes and returns all parts, laid end to end along the dimension named above; each array names one. Nothing has to cross between parts.
Inputs may be any that keep to these rules, and one draw needn't show every extreme that they name: `tile_blocks`: in each row the first tile_count entries are distinct particle blocks, and every particle block appears among the used entries of some row.
All inputs are finite; a program needn't handle non-finite values.
Results may differ from a plain program's by a relative error of at most 0.0033.
Values may be sent and summed in bfloat16 or wider, within the bound.
A program may use at most 128 MiB of HBM per device.

v0:
```python
import math
import jax
import jax.numpy as jnp
from jax import lax
from jax.sharding import PartitionSpec as P

K = 2048
NSH = 16
TILE = 128
MOST = 6
very_negative = -1e30


def merged(array, axis, combine):
    everything = jax.tree.map(lambda part: lax.all_gather(part, axis), array)
    leading = jax.tree.map(lambda part: part[0], everything)

    def turn(k, so_far):
        return combine(so_far, jax.tree.map(lambda part: part[k], everything))

    return lax.fori_loop(1, lax.axis_size(axis), turn, leading)


def shift_phases(window_start):
    half_width = K // 2
    freq_index = jnp.arange(half_width, dtype=jnp.int32)
    freq_x = (freq_index % 32).astype(jnp.float32)
    freq_y = (freq_index // 32 - K // 128).astype(jnp.float32)
    grid_index = window_start + jnp.arange(NSH, dtype=jnp.int32)
    delta_x = (grid_index - 16).astype(jnp.float32) * 0.5
    delta_y = (5 * grid_index % 7 - 3).astype(jnp.float32) * 0.5
    angles = (
        2.0
        * math.pi
        / 64.0
        * (delta_x[:, None] * freq_x[None, :] + delta_y[:, None] * freq_y[None, :])
    )
    return (jnp.cos(angles), jnp.sin(angles))


def shifted_images(image_block, window_start):
    cosine_table, sine_table = shift_phases(window_start)
    half_width = K // 2
    real_part = image_block[:, :half_width].astype(jnp.float32)[None]
    imag_part = image_block[:, half_width:].astype(jnp.float32)[None]
    new_real = real_part * cosine_table[:, None, :] - imag_part * sine_table[:, None, :]
    new_imag = real_part * sine_table[:, None, :] + imag_part * cosine_table[:, None, :]
    stacked = jnp.concatenate([new_real, new_imag], axis=2).astype(jnp.bfloat16)
    return stacked.reshape(NSH * image_block.shape[0], K)


def tile_scores(shifted, ref_block, ref_norms):
    products = lax.dot_general(
        shifted, ref_block, (((1,), (1,)), ((), ())), preferred_element_type=jnp.float32
    )
    return (products - 0.5 * ref_norms[None, :]) / math.sqrt(K)


def combine_stats(first_pair, second_pair):
    top_first, sum_first = first_pair
    top_second, sum_second = second_pair
    top_joint = jnp.maximum(top_first, top_second)
    return (
        top_joint,
        sum_first * jnp.exp(top_first - top_joint) + sum_second * jnp.exp(top_second - top_joint),
    )


def body(particles, references, tile_blocks, tile_count, shift_start):
    local_rows = particles.shape[0]
    axis_count = lax.axis_size("orient")
    my_index = lax.axis_index("orient")
    total_rows = local_rows * axis_count
    block_total = total_rows // TILE
    ref_stack = references[None]
    lower_count = tile_count[my_index]
    ref_norms = jnp.sum(ref_stack.astype(jnp.float32) ** 2, axis=2)
    gathered = lax.all_gather(particles, "orient", axis=0, tiled=True)
    by_block = gathered.reshape(TILE, block_total, K)

    def fetch_block(block_id):
        return lax.dynamic_index_in_dim(by_block, block_id, 1, keepdims=False)

    def describe(item_index):
        in_lower = item_index < lower_count
        column = jnp.where(in_lower, my_index, my_index)
        slot_index = jnp.where(in_lower, item_index, item_index - lower_count)
        which_ref = jnp.where(column == my_index, 0, 1)
        block_id = tile_blocks[column, slot_index]
        image_block = fetch_block(block_id)
        shifted = shifted_images(image_block, shift_start[column, slot_index])
        return (which_ref, block_id, shifted)

    def first_pass(item_index, loop_state):
        score_store, running_top, running_sum = loop_state
        which_ref, block_id, shifted = describe(item_index)
        ref_block = lax.dynamic_index_in_dim(ref_stack, which_ref, 0, keepdims=False)
        norms = lax.dynamic_index_in_dim(ref_norms, which_ref, 0, keepdims=False)
        scores = tile_scores(shifted, ref_block, norms)
        by_particle = scores.reshape(NSH, TILE, TILE)
        tile_top = jnp.max(by_particle, axis=(0, 2))
        old_top = lax.dynamic_index_in_dim(running_top, block_id, 1, keepdims=False)
        old_sum = lax.dynamic_index_in_dim(running_sum, block_id, 1, keepdims=False)
        new_top = jnp.maximum(old_top, tile_top)
        tile_sum = jnp.sum(jnp.exp(by_particle - new_top[None, :, None]), axis=(0, 2))
        new_sum = old_sum * jnp.exp(old_top - new_top) + tile_sum
        running_top = lax.dynamic_update_index_in_dim(running_top, new_top, block_id, 1)
        running_sum = lax.dynamic_update_index_in_dim(running_sum, new_sum, block_id, 1)
        score_store = lax.dynamic_update_index_in_dim(score_store, scores, item_index, 0)
        return (score_store, running_top, running_sum)

    start_state = (
        jnp.zeros((MOST, NSH * TILE, TILE), jnp.float32),
        jnp.full((TILE, block_total), very_negative, jnp.float32),
        jnp.zeros((TILE, block_total), jnp.float32),
    )
    score_store, running_top, running_sum = lax.fori_loop(0, lower_count, first_pass, start_state)
    global_top, global_sum = merged((running_top, running_sum), "orient", combine_stats)

    def second_pass(item_index, loop_state):
        update_acc, weight_acc = loop_state
        which_ref, block_id, shifted = describe(item_index)
        particle_top = lax.dynamic_index_in_dim(global_top, block_id, 1, keepdims=False)
        particle_sum = lax.dynamic_index_in_dim(global_sum, block_id, 1, keepdims=False)
        item_scores = lax.dynamic_index_in_dim(score_store, item_index, 0, keepdims=False).reshape(
            NSH, TILE, TILE
        )
        weights = (
            jnp.exp(item_scores - particle_top[None, :, None]) / particle_sum[None, :, None]
        ).astype(jnp.bfloat16)
        weights = weights.reshape(NSH * TILE, TILE)
        update = lax.dot_general(
            weights, shifted, (((0,), (0,)), ((), ())), preferred_element_type=jnp.float32
        )
        weight_total = jnp.sum(weights.astype(jnp.float32), axis=0)
        current = lax.dynamic_index_in_dim(update_acc, which_ref, 0, keepdims=False)
        update_acc = lax.dynamic_update_index_in_dim(update_acc, current + update, which_ref, 0)
        current_weight = lax.dynamic_index_in_dim(weight_acc, which_ref, 0, keepdims=False)
        weight_acc = lax.dynamic_update_index_in_dim(
            weight_acc, current_weight + weight_total, which_ref, 0
        )
        return (update_acc, weight_acc)

    stack_depth = ref_stack.shape[0]
    back_state = (
        jnp.zeros((stack_depth, TILE, K), jnp.float32),
        jnp.zeros((stack_depth, TILE), jnp.float32),
    )
    update_acc, weight_acc = lax.fori_loop(0, lower_count, second_pass, back_state)
    ref_update = update_acc[0]
    weight_sum = weight_acc[0]
    evidence = (global_top + jnp.log(global_sum)).reshape(total_rows)
    log_evidence = lax.dynamic_slice_in_dim(evidence, my_index * local_rows, local_rows, 0)
    return (ref_update, weight_sum, log_evidence)


def solution(mesh):
    in_specs = (
        P(("grp", "orient"), None),
        P(("grp", "orient"), None),
        P("grp", None),
        P("grp"),
        P("grp", None),
    )
    out_specs = (P(("grp", "orient"), None), P(("grp", "orient")), P(("grp", "orient")))
    return jax.shard_map(body, mesh=mesh, in_specs=in_specs, out_specs=out_specs, check_vma=False)
```

profile of v0, /device:TPU:30, one launch (start us, length us, event | category | flops | bytes accessed | tf_op | source)
XLA Modules:
  0.0 364.0 jit_solution(5189252617112790068)
XLA Ops:
  10.4 48.7 %all-gather.4.cloned.1.call-done = bf16[1024,2048]{1,0:T(8,128)(2,1)} async-done(((bf16[64,2048]{1,0:T(8,128)(2,1)}), bf16[1024,2048]{1,0:T(8,128)(2,1)}) %all-gather.4.cloned.1.call-update) | async-done | bytes 4194320 | tf_op jit(solution)/shard_map/all_gather | solution.py:78
  59.1 6.6 %copy.16 = bf16[128,8,2048]{2,0,1:T(8,128)(2,1)} copy(bf16[128,8,2048]{2,1,0:T(8,128)(2,1)} %bitcast.141) | data formatting | bytes 8388608 | tf_op jit(solution)/shard_map/while | solution.py:117
  65.6 3.4 broadcast_in_dim.45
  69.1 127.2 %while.49 = (s32[]{:T(128)}, f32[6,2048,128]{1,2,0:T(8,128)}, f32[128,8]{0,1:T(8,128)S(1)}, f32[128,8]{0,1:T(8,128)S(1)}, s32[]{:T(128)}, /*index=5*/s32[16,6]{0...) while((s32[]{:T(128)}, f32[6,2048,128]{1,2,0:T(8,128)}, ...), condition=%wide.region_6.7_spmd, body=%wide.region_1.6_spmd.sunk | while | flops 1108950784 | bytes 25503828 | solution.py:117
  77.6 4.8 %subtract_convert_fusion.4 = (bf16[16,128,1024]{2,1,0:T(8,128)(2,1)}, bf16[16,128,1024]{2,1,0:T(8,128)(2,1)}) fusion(f32[16,1024]{1,0:T(8,128)S(1)} %get-tuple-element.877, f32[128,1024]{1,0:T(8,128)S(1)} %get-tuple-element.878, f32[16,1024]{1,0:T(8,128)S(1)} %get-tuple-element.879, f32[128,1024]{1,0:T(8,128)S(1)} %get-tuple-element.880), kind=kLoop, calls=%fused_computation.5.clone.1 | loop fusion | flops 16777216 | bytes 9568256 | tf_op jit(solution)/shard_map/convert.3
  82.4 7.3 %bitcast_dynamic-update-slice_fusion.2 = (f32[6,2048,128]{1,2,0:T(8,128)}, f32[2048,128]{0,1:T(8,128)S(1)}) fusion(f32[6,2048,128]{1,2,0:T(8,128)} %get-tuple-element.934, s32[]{:T(128)S(6)} %select_n.243, f32[128]{0:T(128)S(1)} %multiply_bitcast_fusion.2, bf16[1,128,2048]{2,1,0:T(8,128)(2,1)S(1)} %get-tuple-element.958, ...), kind=kOutput, calls=%fused_computation.8.clone.1 | convolution fusion | flops 1091043328 | bytes 11010564 | tf_op jit(solution)/shard_map/while/body/dot_general | solution.py:53
  98.7 4.8 %subtract_convert_fusion.4 = (bf16[16,128,1024]{2,1,0:T(8,128)(2,1)}, bf16[16,128,1024]{2,1,0:T(8,128)(2,1)}) fusion(f32[16,1024]{1,0:T(8,128)S(1)} %get-tuple-element.877, f32[128,1024]{1,0:T(8,128)S(1)} %get-tuple-element.878, f32[16,1024]{1,0:T(8,128)S(1)} %get-tuple-element.879, f32[128,1024]{1,0:T(8,128)S(1)} %get-tuple-element.880), kind=kLoop, calls=%fused_computation.5.clone.1 | loop fusion | flops 16777216 | bytes 9568256 | tf_op jit(solution)/shard_map/convert.3
  103.5 7.4 %bitcast_dynamic-update-slice_fusion.2 = (f32[6,2048,128]{1,2,0:T(8,128)}, f32[2048,128]{0,1:T(8,128)S(1)}) fusion(f32[6,2048,128]{1,2,0:T(8,128)} %get-tuple-element.934, s32[]{:T(128)S(6)} %select_n.243, f32[128]{0:T(128)S(1)} %multiply_bitcast_fusion.2, bf16[1,128,2048]{2,1,0:T(8,128)(2,1)S(1)} %get-tuple-element.958, ...), kind=kOutput, calls=%fused_computation.8.clone.1 | convolution fusion | flops 1091043328 | bytes 11010564 | tf_op jit(solution)/shard_map/while/body/dot_general | solution.py:53
  119.8 4.8 %subtract_convert_fusion.4 = (bf16[16,128,1024]{2,1,0:T(8,128)(2,1)}, bf16[16,128,1024]{2,1,0:T(8,128)(2,1)}) fusion(f32[16,1024]{1,0:T(8,128)S(1)} %get-tuple-element.877, f32[128,1024]{1,0:T(8,128)S(1)} %get-tuple-element.878, f32[16,1024]{1,0:T(8,128)S(1)} %get-tuple-element.879, f32[128,1024]{1,0:T(8,128)S(1)} %get-tuple-element.880), kind=kLoop, calls=%fused_computation.5.clone.1 | loop fusion | flops 16777216 | bytes 9568256 | tf_op jit(solution)/shard_map/convert.3
  124.6 7.4 %bitcast_dynamic-update-slice_fusion.2 = (f32[6,2048,128]{1,2,0:T(8,128)}, f32[2048,128]{0,1:T(8,128)S(1)}) fusion(f32[6,2048,128]{1,2,0:T(8,128)} %get-tuple-element.934, s32[]{:T(128)S(6)} %select_n.243, f32[128]{0:T(128)S(1)} %multiply_bitcast_fusion.2, bf16[1,128,2048]{2,1,0:T(8,128)(2,1)S(1)} %get-tuple-element.958, ...), kind=kOutput, calls=%fused_computation.8.clone.1 | convolution fusion | flops 1091043328 | bytes 11010564 | tf_op jit(solution)/shard_map/while/body/dot_general | solution.py:53
  140.9 4.8 %subtract_convert_fusion.4 = (bf16[16,128,1024]{2,1,0:T(8,128)(2,1)}, bf16[16,128,1024]{2,1,0:T(8,128)(2,1)}) fusion(f32[16,1024]{1,0:T(8,128)S(1)} %get-tuple-element.877, f32[128,1024]{1,0:T(8,128)S(1)} %get-tuple-element.878, f32[16,1024]{1,0:T(8,128)S(1)} %get-tuple-element.879, f32[128,1024]{1,0:T(8,128)S(1)} %get-tuple-element.880), kind=kLoop, calls=%fused_computation.5.clone.1 | loop fusion | flops 16777216 | bytes 9568256 | tf_op jit(solution)/shard_map/convert.3
  145.7 7.3 %bitcast_dynamic-update-slice_fusion.2 = (f32[6,2048,128]{1,2,0:T(8,128)}, f32[2048,128]{0,1:T(8,128)S(1)}) fusion(f32[6,2048,128]{1,2,0:T(8,128)} %get-tuple-element.934, s32[]{:T(128)S(6)} %select_n.243, f32[128]{0:T(128)S(1)} %multiply_bitcast_fusion.2, bf16[1,128,2048]{2,1,0:T(8,128)(2,1)S(1)} %get-tuple-element.958, ...), kind=kOutput, calls=%fused_computation.8.clone.1 | convolution fusion | flops 1091043328 | bytes 11010564 | tf_op jit(solution)/shard_map/while/body/dot_general | solution.py:53
  162.0 4.8 %subtract_convert_fusion.4 = (bf16[16,128,1024]{2,1,0:T(8,128)(2,1)}, bf16[16,128,1024]{2,1,0:T(8,128)(2,1)}) fusion(f32[16,1024]{1,0:T(8,128)S(1)} %get-tuple-element.877, f32[128,1024]{1,0:T(8,128)S(1)} %get-tuple-element.878, f32[16,1024]{1,0:T(8,128)S(1)} %get-tuple-element.879, f32[128,1024]{1,0:T(8,128)S(1)} %get-tuple-element.880), kind=kLoop, calls=%fused_computation.5.clone.1 | loop fusion | flops 16777216 | bytes 9568256 | tf_op jit(solution)/shard_map/convert.3
  166.8 7.4 %bitcast_dynamic-update-slice_fusion.2 = (f32[6,2048,128]{1,2,0:T(8,128)}, f32[2048,128]{0,1:T(8,128)S(1)}) fusion(f32[6,2048,128]{1,2,0:T(8,128)} %get-tuple-element.934, s32[]{:T(128)S(6)} %select_n.243, f32[128]{0:T(128)S(1)} %multiply_bitcast_fusion.2, bf16[1,128,2048]{2,1,0:T(8,128)(2,1)S(1)} %get-tuple-element.958, ...), kind=kOutput, calls=%fused_computation.8.clone.1 | convolution fusion | flops 1091043328 | bytes 11010564 | tf_op jit(solution)/shard_map/while/body/dot_general | solution.py:53
  183.0 4.8 %subtract_convert_fusion.4 = (bf16[16,128,1024]{2,1,0:T(8,128)(2,1)}, bf16[16,128,1024]{2,1,0:T(8,128)(2,1)}) fusion(f32[16,1024]{1,0:T(8,128)S(1)} %get-tuple-element.877, f32[128,1024]{1,0:T(8,128)S(1)} %get-tuple-element.878, f32[16,1024]{1,0:T(8,128)S(1)} %get-tuple-element.879, f32[128,1024]{1,0:T(8,128)S(1)} %get-tuple-element.880), kind=kLoop, calls=%fused_computation.5.clone.1 | loop fusion | flops 16777216 | bytes 9568256 | tf_op jit(solution)/shard_map/convert.3
  187.8 7.4 %bitcast_dynamic-update-slice_fusion.2 = (f32[6,2048,128]{1,2,0:T(8,128)}, f32[2048,128]{0,1:T(8,128)S(1)}) fusion(f32[6,2048,128]{1,2,0:T(8,128)} %get-tuple-element.934, s32[]{:T(128)S(6)} %select_n.243, f32[128]{0:T(128)S(1)} %multiply_bitcast_fusion.2, bf16[1,128,2048]{2,1,0:T(8,128)(2,1)S(1)} %get-tuple-element.958, ...), kind=kOutput, calls=%fused_computation.8.clone.1 | convolution fusion | flops 1091043328 | bytes 11010564 | tf_op jit(solution)/shard_map/while/body/dot_general | solution.py:53
  196.3 16.7 %all-gather = f32[2048,8]{0,1:T(8,128)S(1)} all-gather(f32[128,8]{0,1:T(8,128)S(1)} %get-tuple-element.540), channel_id=2, replica_groups=mesh['grp'=2,'orient'=16] {'orient'}, dimensions={0}, use_global_device_ids=true | all-gather | bytes 69632 | tf_op jit(solution)/shard_map/all_gather | solution.py:15
  212.9 19.8 %all-gather.1 = f32[2048,8]{0,1:T(8,128)S(1)} all-gather(f32[128,8]{0,1:T(8,128)S(1)} %get-tuple-element.541), channel_id=3, replica_groups=mesh['grp'=2,'orient'=16] {'orient'}, dimensions={0}, use_global_device_ids=true | all-gather | bytes 69632 | tf_op jit(solution)/shard_map/all_gather | solution.py:15
  233.7 122.5 %while.51 = (s32[]{:T(128)}, f32[1,128,2048]{2,1,0:T(8,128)S(1)}, f32[1,128]{1,0:T(1,128)S(1)}, s32[]{:T(128)}, f32[6,2048,128]{1,2,0:T(8,128)}, /*index=5*/s32[...) while((s32[]{:T(128)}, f32[1,128,2048]{2,1,0:T(8,128)S(1)}, ...), condition=%wide.region_11.12_spmd, body=%wide.region_9.11_spmd.sunk | while | flops 1109998848 | bytes 29153852 | solution.py:149
  242.2 4.8 %subtract_convert_fusion.5 = (bf16[16,128,1024]{2,1,0:T(8,128)(2,1)}, bf16[16,128,1024]{2,1,0:T(8,128)(2,1)}) fusion(f32[16,1024]{1,0:T(8,128)S(1)} %get-tuple-element.909, f32[128,1024]{1,0:T(8,128)S(1)} %get-tuple-element.910, f32[16,1024]{1,0:T(8,128)S(1)} %get-tuple-element.911, f32[128,1024]{1,0:T(8,128)S(1)} %get-tuple-element.912), kind=kLoop, calls=%fused_computation.57.clone.1 | loop fusion | flops 16777216 | bytes 9568256 | tf_op jit(solution)/shard_map/convert.4
  247.0 1.3 constant_dynamic-slice_fusion.6
  248.7 4.6 %fusion.84 = f32[1,128,2048]{2,1,0:T(8,128)S(1)} fusion(bf16[16,128,1024]{2,1,0:T(8,128)(2,1)} %get-tuple-element.913, bf16[16,128,1024]{2,1,0:T(8,128)(2,1)} %get-tuple-element.914, f32[1,128,2048]{2,1,0:T(8,128)S(1)} %get-tuple-element.1005, f32[16,128,128]{2,1,0:T(8,128)S(1)} %bitcast.140, f32[128]{0:T(128)S(1)} %get-tuple-element.915, ...), kind=kOutput, calls=%fused_computation.60.clone.1 | convolution fusion | flops 1091567616 | bytes 11535360 | tf_op jit(solution)/shard_map/while/body/dot_general | solution.py:132
  262.6 4.8 %subtract_convert_fusion.5 = (bf16[16,128,1024]{2,1,0:T(8,128)(2,1)}, bf16[16,128,1024]{2,1,0:T(8,128)(2,1)}) fusion(f32[16,1024]{1,0:T(8,128)S(1)} %get-tuple-element.909, f32[128,1024]{1,0:T(8,128)S(1)} %get-tuple-element.910, f32[16,1024]{1,0:T(8,128)S(1)} %get-tuple-element.911, f32[128,1024]{1,0:T(8,128)S(1)} %get-tuple-element.912), kind=kLoop, calls=%fused_computation.57.clone.1 | loop fusion | flops 16777216 | bytes 9568256 | tf_op jit(solution)/shard_map/convert.4
  269.0 4.6 %fusion.84 = f32[1,128,2048]{2,1,0:T(8,128)S(1)} fusion(bf16[16,128,1024]{2,1,0:T(8,128)(2,1)} %get-tuple-element.913, bf16[16,128,1024]{2,1,0:T(8,128)(2,1)} %get-tuple-element.914, f32[1,128,2048]{2,1,0:T(8,128)S(1)} %get-tuple-element.1005, f32[16,128,128]{2,1,0:T(8,128)S(1)} %bitcast.140, f32[128]{0:T(128)S(1)} %get-tuple-element.915, ...), kind=kOutput, calls=%fused_computation.60.clone.1 | convolution fusion | flops 1091567616 | bytes 11535360 | tf_op jit(solution)/shard_map/while/body/dot_general | solution.py:132
  282.9 4.8 %subtract_convert_fusion.5 = (bf16[16,128,1024]{2,1,0:T(8,128)(2,1)}, bf16[16,128,1024]{2,1,0:T(8,128)(2,1)}) fusion(f32[16,1024]{1,0:T(8,128)S(1)} %get-tuple-element.909, f32[128,1024]{1,0:T(8,128)S(1)} %get-tuple-element.910, f32[16,1024]{1,0:T(8,128)S(1)} %get-tuple-element.911, f32[128,1024]{1,0:T(8,128)S(1)} %get-tuple-element.912), kind=kLoop, calls=%fused_computation.57.clone.1 | loop fusion | flops 16777216 | bytes 9568256 | tf_op jit(solution)/shard_map/convert.4
  289.3 4.6 %fusion.84 = f32[1,128,2048]{2,1,0:T(8,128)S(1)} fusion(bf16[16,128,1024]{2,1,0:T(8,128)(2,1)} %get-tuple-element.913, bf16[16,128,1024]{2,1,0:T(8,128)(2,1)} %get-tuple-element.914, f32[1,128,2048]{2,1,0:T(8,128)S(1)} %get-tuple-element.1005, f32[16,128,128]{2,1,0:T(8,128)S(1)} %bitcast.140, f32[128]{0:T(128)S(1)} %get-tuple-element.915, ...), kind=kOutput, calls=%fused_computation.60.clone.1 | convolution fusion | flops 1091567616 | bytes 11535360 | tf_op jit(solution)/shard_map/while/body/dot_general | solution.py:132
  303.2 4.8 %subtract_convert_fusion.5 = (bf16[16,128,1024]{2,1,0:T(8,128)(2,1)}, bf16[16,128,1024]{2,1,0:T(8,128)(2,1)}) fusion(f32[16,1024]{1,0:T(8,128)S(1)} %get-tuple-element.909, f32[128,1024]{1,0:T(8,128)S(1)} %get-tuple-element.910, f32[16,1024]{1,0:T(8,128)S(1)} %get-tuple-element.911, f32[128,1024]{1,0:T(8,128)S(1)} %get-tuple-element.912), kind=kLoop, calls=%fused_computation.57.clone.1 | loop fusion | flops 16777216 | bytes 9568256 | tf_op jit(solution)/shard_map/convert.4
  309.6 4.6 %fusion.84 = f32[1,128,2048]{2,1,0:T(8,128)S(1)} fusion(bf16[16,128,1024]{2,1,0:T(8,128)(2,1)} %get-tuple-element.913, bf16[16,128,1024]{2,1,0:T(8,128)(2,1)} %get-tuple-element.914, f32[1,128,2048]{2,1,0:T(8,128)S(1)} %get-tuple-element.1005, f32[16,128,128]{2,1,0:T(8,128)S(1)} %bitcast.140, f32[128]{0:T(128)S(1)} %get-tuple-element.915, ...), kind=kOutput, calls=%fused_computation.60.clone.1 | convolution fusion | flops 1091567616 | bytes 11535360 | tf_op jit(solution)/shard_map/while/body/dot_general | solution.py:132
  323.5 4.8 %subtract_convert_fusion.5 = (bf16[16,128,1024]{2,1,0:T(8,128)(2,1)}, bf16[16,128,1024]{2,1,0:T(8,128)(2,1)}) fusion(f32[16,1024]{1,0:T(8,128)S(1)} %get-tuple-element.909, f32[128,1024]{1,0:T(8,128)S(1)} %get-tuple-element.910, f32[16,1024]{1,0:T(8,128)S(1)} %get-tuple-element.911, f32[128,1024]{1,0:T(8,128)S(1)} %get-tuple-element.912), kind=kLoop, calls=%fused_computation.57.clone.1 | loop fusion | flops 16777216 | bytes 9568256 | tf_op jit(solution)/shard_map/convert.4
  329.9 4.6 %fusion.84 = f32[1,128,2048]{2,1,0:T(8,128)S(1)} fusion(bf16[16,128,1024]{2,1,0:T(8,128)(2,1)} %get-tuple-element.913, bf16[16,128,1024]{2,1,0:T(8,128)(2,1)} %get-tuple-element.914, f32[1,128,2048]{2,1,0:T(8,128)S(1)} %get-tuple-element.1005, f32[16,128,128]{2,1,0:T(8,128)S(1)} %bitcast.140, f32[128]{0:T(128)S(1)} %get-tuple-element.915, ...), kind=kOutput, calls=%fused_computation.60.clone.1 | convolution fusion | flops 1091567616 | bytes 11535360 | tf_op jit(solution)/shard_map/while/body/dot_general | solution.py:132
  343.8 4.8 %subtract_convert_fusion.5 = (bf16[16,128,1024]{2,1,0:T(8,128)(2,1)}, bf16[16,128,1024]{2,1,0:T(8,128)(2,1)}) fusion(f32[16,1024]{1,0:T(8,128)S(1)} %get-tuple-element.909, f32[128,1024]{1,0:T(8,128)S(1)} %get-tuple-element.910, f32[16,1024]{1,0:T(8,128)S(1)} %get-tuple-element.911, f32[128,1024]{1,0:T(8,128)S(1)} %get-tuple-element.912), kind=kLoop, calls=%fused_computation.57.clone.1 | loop fusion | flops 16777216 | bytes 9568256 | tf_op jit(solution)/shard_map/convert.4
  350.2 4.6 %fusion.84 = f32[1,128,2048]{2,1,0:T(8,128)S(1)} fusion(bf16[16,128,1024]{2,1,0:T(8,128)(2,1)} %get-tuple-element.913, bf16[16,128,1024]{2,1,0:T(8,128)(2,1)} %get-tuple-element.914, f32[1,128,2048]{2,1,0:T(8,128)S(1)} %get-tuple-element.1005, f32[16,128,128]{2,1,0:T(8,128)S(1)} %bitcast.140, f32[128]{0:T(128)S(1)} %get-tuple-element.915, ...), kind=kOutput, calls=%fused_computation.60.clone.1 | convolution fusion | flops 1091567616 | bytes 11535360 | tf_op jit(solution)/shard_map/while/body/dot_general | solution.py:132
  (221 shorter events, 76.9 us)
Async XLA Ops:
  7.2 51.9 %all-gather.4.cloned.1.call-start = ((), (), s32[]{:S(2)}) async-start(), calls=%async_computation | async-start | bytes 4456448 | tf_op jit(solution)/shard_map/all_gather | solution.py:78
  59.1 10.0 %copy-start.1 = (bf16[128,2048]{1,0:T(8,128)(2,1)S(1)}, bf16[128,2048]{1,0:T(8,128)(2,1)}, u32[]{:S(2)}) copy-start(bf16[128,2048]{1,0:T(8,128)(2,1)} %param.12) | copy-start | bytes 1572868
  356.2 1.0 copy-start
  356.2 1.0 copy-start.2
Sparse Core Ops, SparseCore 0:
  10.1 48.8 all-gather.3
where the time goes:
time: 366 us; the launch traced here: 364 us
  other arithmetic  77.9 us (21%)
  matrix products  71.5 us (20%)
  local copies, waits for them, and re-layouts  66.5 us (18%)
  waiting for transfers between devices  49.4 us (13%)
  loops' own time  48.1 us (13%)
  blocking collectives  36.5 us (10%)
  between operations  14.1 us (4%)
    another operation x12, other arithmetic  57.5 us
    all_gather x1, waiting for transfers between devices, body(): gathered = lax.all_gather(particles, 'orient', axis=0, tiled=True)  48.7 us
    dot_general x6, matrix products, tile_scores(): lax.dot_general(shifted, ref_block, (((1,), (1,)), ((), ())), preferred_e...  44.2 us
    all_gather x2, blocking collectives, merged(): everything = jax.tree.map(lambda part: lax.all_gather(part, axis), array)  36.5 us
    dot_general x6, matrix products, second_pass(): lax.dot_general(weights, shifted, (((0,), (0,)), ((), ())), preferred_ele...  27.3 us
    another operation x1, loops' own time, body(): lax.fori_loop(0, lower_count, second_pass, back_state)  24 us
    another operation x1, loops' own time, body(): lax.fori_loop(0, lower_count, first_pass, start_state)  23.8 us
    dynamic_slice x12, local copies, waits for them, and re-layouts, describe(): block_id = tile_blocks[column, slot_index]  15.4 us
  transfers between devices with their start and end apart: 1, of which 1 were waited for; matrix products, arithmetic and copies ran while one was open for 1% of the time, Pallas kernels for 0%

commit v1 on v0

--- a/solution.py
+++ b/solution.py
@@ -75,7 +75,9 @@
     ref_stack = references[None]
     lower_count = tile_count[my_index]
     ref_norms = jnp.sum(ref_stack.astype(jnp.float32) ** 2, axis=2)
-    gathered = lax.all_gather(particles, "orient", axis=0, tiled=True)
+    gathered = jnp.concatenate(
+        lax.all_to_all(jnp.stack([particles] * lax.axis_size("orient")), "orient", 0, 0), axis=0
+    )
     by_block = gathered.reshape(TILE, block_total, K)
 
     def fetch_block(block_id):

time: 366 us -> 402 us (1.098)
  waiting for transfers between devices: 49.4 us -> 90.4 us
  between operations: 14.1 us -> 0.72 us
  starting transfers between devices: 0.04 us -> 6.02 us
    all_to_all x0 -> x1, waiting for transfers between devices: none -> 90.4 us  [body(): lax.all_to_all(jnp.stack([particles] * lax.axis_size('orient')), 'orient'...]
    all_gather x1 -> x0, waiting for transfers between devices: 48.7 us -> none  [body(): gathered = lax.all_gather(particles, 'orient', axis=0, tiled=True)]
    all_to_all x0 -> x1, starting transfers between devices: none -> 6.02 us  [body(): lax.all_to_all(jnp.stack([particles] * lax.axis_size('orient')), 'orient'...]
  transfers between devices with their start and end apart: 1 -> 1, of which waited for: 1 -> 1; matrix products, arithmetic and copies ran while one was open for 1% -> 0% of each run, Pallas kernels for 0% -> 0%
where the time goes in v1:
time: 402 us; the launch traced here: 400 us
  waiting for transfers between devices  90.4 us (22%)
  other arithmetic  76.8 us (19%)
  matrix products  71.5 us (18%)
  local copies, waits for them, and re-layouts  69.3 us (17%)
  loops' own time  48.3 us (12%)
  blocking collectives  36.5 us (9%)
  starting transfers between devices  6.02 us (1%)
    all_to_all x1, waiting for transfers between devices, body(): lax.all_to_all(jnp.stack([particles] * lax.axis_size('orient')), 'orient'...  90.4 us
    another operation x12, other arithmetic  57.5 us
    dot_general x6, matrix products, tile_scores(): lax.dot_general(shifted, ref_block, (((1,), (1,)), ((), ())), preferred_e...  44.2 us
    all_gather x2, blocking collectives, merged(): everything = jax.tree.map(lambda part: lax.all_gather(part, axis), array)  36.5 us
    dot_general x6, matrix products, second_pass(): lax.dot_general(weights, shifted, (((0,), (0,)), ((), ())), preferred_ele...  27.3 us
    another operation x1, loops' own time, body(): lax.fori_loop(0, lower_count, second_pass, back_state)  24.1 us
    another operation x1, loops' own time, body(): lax.fori_loop(0, lower_count, first_pass, start_state)  23.8 us
    dynamic_slice x12, local copies, waits for them, and re-layouts, describe(): block_id = tile_blocks[column, slot_index]  15.4 us
  transfers between devices with their start and end apart: 1, of which 1 were waited for; matrix products, arithmetic and copies ran while one was open for 0% of the time, Pallas kernels for 0%

profile of v1, /device:TPU:30, one launch (start us, length us, event | category | flops | bytes accessed | tf_op | source)
XLA Modules:
  0.0 399.6 jit_solution(11844682483697092943)
XLA Ops:
  0.7 3.5 stack.2
  4.2 6.0 %all-to-all-start = ((bf16[16,64,2048]{2,1,0:T(8,128)(2,1)}), bf16[16,64,2048]{2,1,0:T(8,128)(2,1)}, u32[]{:S(2)}, u32[]{:S(2)}) async-start(bf16[16,64,2048]{2,1,0:T(8,128)(2,1)} %stack.2), calls=%async_computation | async-start | bytes 8388608 | tf_op jit(solution)/shard_map/all_to_all | solution.py:79
  11.0 90.4 %all-to-all-done = bf16[16,64,2048]{2,1,0:T(8,128)(2,1)} async-done(((bf16[16,64,2048]{2,1,0:T(8,128)(2,1)}), bf16[16,64,2048]{2,1,0:T(8,128)(2,1)}, u32[]{:S(2)}, u32[]{:S(2)}) %all-to-all-start) | async-done | bytes 4194336 | tf_op jit(solution)/shard_map/all_to_all | solution.py:79
  101.4 6.5 %copy.16 = bf16[128,8,2048]{2,0,1:T(8,128)(2,1)} copy(bf16[128,8,2048]{2,1,0:T(8,128)(2,1)} %bitcast.30) | data formatting | bytes 8388608 | tf_op jit(solution)/shard_map/while | solution.py:119
  111.3 127.2 %while.49 = (s32[]{:T(128)}, f32[6,2048,128]{1,2,0:T(8,128)}, f32[128,8]{0,1:T(8,128)S(1)}, f32[128,8]{0,1:T(8,128)S(1)}, s32[]{:T(128)}, /*index=5*/s32[16,6]{0...) while((s32[]{:T(128)}, f32[6,2048,128]{1,2,0:T(8,128)}, ...), condition=%wide.region_6.7_spmd, body=%wide.region_1.6_spmd.sunk | while | flops 1108950784 | bytes 25503828 | solution.py:119
  119.9 4.8 %subtract_convert_fusion.4 = (bf16[16,128,1024]{2,1,0:T(8,128)(2,1)}, bf16[16,128,1024]{2,1,0:T(8,128)(2,1)}) fusion(f32[16,1024]{1,0:T(8,128)S(1)} %get-tuple-element.877, f32[128,1024]{1,0:T(8,128)S(1)} %get-tuple-element.878, f32[16,1024]{1,0:T(8,128)S(1)} %get-tuple-element.879, f32[128,1024]{1,0:T(8,128)S(1)} %get-tuple-element.880), kind=kLoop, calls=%fused_computation.5.clone.1 | loop fusion | flops 16777216 | bytes 9568256 | tf_op jit(solution)/shard_map/convert.3
  124.7 7.3 %bitcast_dynamic-update-slice_fusion.2 = (f32[6,2048,128]{1,2,0:T(8,128)}, f32[2048,128]{0,1:T(8,128)S(1)}) fusion(f32[6,2048,128]{1,2,0:T(8,128)} %get-tuple-element.934, s32[]{:T(128)S(6)} %select_n.243, f32[128]{0:T(128)S(1)} %multiply_bitcast_fusion.2, bf16[1,128,2048]{2,1,0:T(8,128)(2,1)S(1)} %get-tuple-element.958, ...), kind=kOutput, calls=%fused_computation.8.clone.1 | convolution fusion | flops 1091043328 | bytes 11010564 | tf_op jit(solution)/shard_map/while/body/dot_general | solution.py:53
  141.0 4.8 %subtract_convert_fusion.4 = (bf16[16,128,1024]{2,1,0:T(8,128)(2,1)}, bf16[16,128,1024]{2,1,0:T(8,128)(2,1)}) fusion(f32[16,1024]{1,0:T(8,128)S(1)} %get-tuple-element.877, f32[128,1024]{1,0:T(8,128)S(1)} %get-tuple-element.878, f32[16,1024]{1,0:T(8,128)S(1)} %get-tuple-element.879, f32[128,1024]{1,0:T(8,128)S(1)} %get-tuple-element.880), kind=kLoop, calls=%fused_computation.5.clone.1 | loop fusion | flops 16777216 | bytes 9568256 | tf_op jit(solution)/shard_map/convert.3
  145.8 7.4 %bitcast_dynamic-update-slice_fusion.2 = (f32[6,2048,128]{1,2,0:T(8,128)}, f32[2048,128]{0,1:T(8,128)S(1)}) fusion(f32[6,2048,128]{1,2,0:T(8,128)} %get-tuple-element.934, s32[]{:T(128)S(6)} %select_n.243, f32[128]{0:T(128)S(1)} %multiply_bitcast_fusion.2, bf16[1,128,2048]{2,1,0:T(8,128)(2,1)S(1)} %get-tuple-element.958, ...), kind=kOutput, calls=%fused_computation.8.clone.1 | convolution fusion | flops 1091043328 | bytes 11010564 | tf_op jit(solution)/shard_map/while/body/dot_general | solution.py:53
  162.1 4.8 %subtract_convert_fusion.4 = (bf16[16,128,1024]{2,1,0:T(8,128)(2,1)}, bf16[16,128,1024]{2,1,0:T(8,128)(2,1)}) fusion(f32[16,1024]{1,0:T(8,128)S(1)} %get-tuple-element.877, f32[128,1024]{1,0:T(8,128)S(1)} %get-tuple-element.878, f32[16,1024]{1,0:T(8,128)S(1)} %get-tuple-element.879, f32[128,1024]{1,0:T(8,128)S(1)} %get-tuple-element.880), kind=kLoop, calls=%fused_computation.5.clone.1 | loop fusion | flops 16777216 | bytes 9568256 | tf_op jit(solution)/shard_map/convert.3
  166.9 7.4 %bitcast_dynamic-update-slice_fusion.2 = (f32[6,2048,128]{1,2,0:T(8,128)}, f32[2048,128]{0,1:T(8,128)S(1)}) fusion(f32[6,2048,128]{1,2,0:T(8,128)} %get-tuple-element.934, s32[]{:T(128)S(6)} %select_n.243, f32[128]{0:T(128)S(1)} %multiply_bitcast_fusion.2, bf16[1,128,2048]{2,1,0:T(8,128)(2,1)S(1)} %get-tuple-element.958, ...), kind=kOutput, calls=%fused_computation.8.clone.1 | convolution fusion | flops 1091043328 | bytes 11010564 | tf_op jit(solution)/shard_map/while/body/dot_general | solution.py:53
  183.2 4.8 %subtract_convert_fusion.4 = (bf16[16,128,1024]{2,1,0:T(8,128)(2,1)}, bf16[16,128,1024]{2,1,0:T(8,128)(2,1)}) fusion(f32[16,1024]{1,0:T(8,128)S(1)} %get-tuple-element.877, f32[128,1024]{1,0:T(8,128)S(1)} %get-tuple-element.878, f32[16,1024]{1,0:T(8,128)S(1)} %get-tuple-element.879, f32[128,1024]{1,0:T(8,128)S(1)} %get-tuple-element.880), kind=kLoop, calls=%fused_computation.5.clone.1 | loop fusion | flops 16777216 | bytes 9568256 | tf_op jit(solution)/shard_map/convert.3
  188.0 7.3 %bitcast_dynamic-update-slice_fusion.2 = (f32[6,2048,128]{1,2,0:T(8,128)}, f32[2048,128]{0,1:T(8,128)S(1)}) fusion(f32[6,2048,128]{1,2,0:T(8,128)} %get-tuple-element.934, s32[]{:T(128)S(6)} %select_n.243, f32[128]{0:T(128)S(1)} %multiply_bitcast_fusion.2, bf16[1,128,2048]{2,1,0:T(8,128)(2,1)S(1)} %get-tuple-element.958, ...), kind=kOutput, calls=%fused_computation.8.clone.1 | convolution fusion | flops 1091043328 | bytes 11010564 | tf_op jit(solution)/shard_map/while/body/dot_general | solution.py:53
  204.2 4.8 %subtract_convert_fusion.4 = (bf16[16,128,1024]{2,1,0:T(8,128)(2,1)}, bf16[16,128,1024]{2,1,0:T(8,128)(2,1)}) fusion(f32[16,1024]{1,0:T(8,128)S(1)} %get-tuple-element.877, f32[128,1024]{1,0:T(8,128)S(1)} %get-tuple-element.878, f32[16,1024]{1,0:T(8,128)S(1)} %get-tuple-element.879, f32[128,1024]{1,0:T(8,128)S(1)} %get-tuple-element.880), kind=kLoop, calls=%fused_computation.5.clone.1 | loop fusion | flops 16777216 | bytes 9568256 | tf_op jit(solution)/shard_map/convert.3
  209.0 7.4 %bitcast_dynamic-update-slice_fusion.2 = (f32[6,2048,128]{1,2,0:T(8,128)}, f32[2048,128]{0,1:T(8,128)S(1)}) fusion(f32[6,2048,128]{1,2,0:T(8,128)} %get-tuple-element.934, s32[]{:T(128)S(6)} %select_n.243, f32[128]{0:T(128)S(1)} %multiply_bitcast_fusion.2, bf16[1,128,2048]{2,1,0:T(8,128)(2,1)S(1)} %get-tuple-element.958, ...), kind=kOutput, calls=%fused_computation.8.clone.1 | convolution fusion | flops 1091043328 | bytes 11010564 | tf_op jit(solution)/shard_map/while/body/dot_general | solution.py:53
  225.3 4.8 %subtract_convert_fusion.4 = (bf16[16,128,1024]{2,1,0:T(8,128)(2,1)}, bf16[16,128,1024]{2,1,0:T(8,128)(2,1)}) fusion(f32[16,1024]{1,0:T(8,128)S(1)} %get-tuple-element.877, f32[128,1024]{1,0:T(8,128)S(1)} %get-tuple-element.878, f32[16,1024]{1,0:T(8,128)S(1)} %get-tuple-element.879, f32[128,1024]{1,0:T(8,128)S(1)} %get-tuple-element.880), kind=kLoop, calls=%fused_computation.5.clone.1 | loop fusion | flops 16777216 | bytes 9568256 | tf_op jit(solution)/shard_map/convert.3
  230.1 7.4 %bitcast_dynamic-update-slice_fusion.2 = (f32[6,2048,128]{1,2,0:T(8,128)}, f32[2048,128]{0,1:T(8,128)S(1)}) fusion(f32[6,2048,128]{1,2,0:T(8,128)} %get-tuple-element.934, s32[]{:T(128)S(6)} %select_n.243, f32[128]{0:T(128)S(1)} %multiply_bitcast_fusion.2, bf16[1,128,2048]{2,1,0:T(8,128)(2,1)S(1)} %get-tuple-element.958, ...), kind=kOutput, calls=%fused_computation.8.clone.1 | convolution fusion | flops 1091043328 | bytes 11010564 | tf_op jit(solution)/shard_map/while/body/dot_general | solution.py:53
  238.5 16.7 %all-gather = f32[2048,8]{0,1:T(8,128)S(1)} all-gather(f32[128,8]{0,1:T(8,128)S(1)} %get-tuple-element.540), channel_id=2, replica_groups=mesh['grp'=2,'orient'=16] {'orient'}, dimensions={0}, use_global_device_ids=true | all-gather | bytes 69632 | tf_op jit(solution)/shard_map/all_gather | solution.py:15
  255.2 19.8 %all-gather.1 = f32[2048,8]{0,1:T(8,128)S(1)} all-gather(f32[128,8]{0,1:T(8,128)S(1)} %get-tuple-element.541), channel_id=3, replica_groups=mesh['grp'=2,'orient'=16] {'orient'}, dimensions={0}, use_global_device_ids=true | all-gather | bytes 69632 | tf_op jit(solution)/shard_map/all_gather | solution.py:15
  276.0 122.6 %while.51 = (s32[]{:T(128)}, f32[1,128,2048]{2,1,0:T(8,128)S(1)}, f32[1,128]{1,0:T(1,128)S(1)}, s32[]{:T(128)}, f32[6,2048,128]{1,2,0:T(8,128)}, /*index=5*/s32[...) while((s32[]{:T(128)}, f32[1,128,2048]{2,1,0:T(8,128)S(1)}, ...), condition=%wide.region_11.12_spmd, body=%wide.region_9.11_spmd.sunk | while | flops 1109998848 | bytes 29153852 | solution.py:151
  284.7 4.8 %subtract_convert_fusion.5 = (bf16[16,128,1024]{2,1,0:T(8,128)(2,1)}, bf16[16,128,1024]{2,1,0:T(8,128)(2,1)}) fusion(f32[16,1024]{1,0:T(8,128)S(1)} %get-tuple-element.909, f32[128,1024]{1,0:T(8,128)S(1)} %get-tuple-element.910, f32[16,1024]{1,0:T(8,128)S(1)} %get-tuple-element.911, f32[128,1024]{1,0:T(8,128)S(1)} %get-tuple-element.912), kind=kLoop, calls=%fused_computation.57.clone.1 | loop fusion | flops 16777216 | bytes 9568256 | tf_op jit(solution)/shard_map/convert.4
  291.1 4.5 %fusion.84 = f32[1,128,2048]{2,1,0:T(8,128)S(1)} fusion(bf16[16,128,1024]{2,1,0:T(8,128)(2,1)} %get-tuple-element.913, bf16[16,128,1024]{2,1,0:T(8,128)(2,1)} %get-tuple-element.914, f32[1,128,2048]{2,1,0:T(8,128)S(1)} %get-tuple-element.1005, f32[16,128,128]{2,1,0:T(8,128)S(1)} %bitcast.140, f32[128]{0:T(128)S(1)} %get-tuple-element.915, ...), kind=kOutput, calls=%fused_computation.60.clone.1 | convolution fusion | flops 1091567616 | bytes 11535360 | tf_op jit(solution)/shard_map/while/body/dot_general | solution.py:134
  305.0 4.8 %subtract_convert_fusion.5 = (bf16[16,128,1024]{2,1,0:T(8,128)(2,1)}, bf16[16,128,1024]{2,1,0:T(8,128)(2,1)}) fusion(f32[16,1024]{1,0:T(8,128)S(1)} %get-tuple-element.909, f32[128,1024]{1,0:T(8,128)S(1)} %get-tuple-element.910, f32[16,1024]{1,0:T(8,128)S(1)} %get-tuple-element.911, f32[128,1024]{1,0:T(8,128)S(1)} %get-tuple-element.912), kind=kLoop, calls=%fused_computation.57.clone.1 | loop fusion | flops 16777216 | bytes 9568256 | tf_op jit(solution)/shard_map/convert.4
  311.4 4.5 %fusion.84 = f32[1,128,2048]{2,1,0:T(8,128)S(1)} fusion(bf16[16,128,1024]{2,1,0:T(8,128)(2,1)} %get-tuple-element.913, bf16[16,128,1024]{2,1,0:T(8,128)(2,1)} %get-tuple-element.914, f32[1,128,2048]{2,1,0:T(8,128)S(1)} %get-tuple-element.1005, f32[16,128,128]{2,1,0:T(8,128)S(1)} %bitcast.140, f32[128]{0:T(128)S(1)} %get-tuple-element.915, ...), kind=kOutput, calls=%fused_computation.60.clone.1 | convolution fusion | flops 1091567616 | bytes 11535360 | tf_op jit(solution)/shard_map/while/body/dot_general | solution.py:134
  325.3 4.8 %subtract_convert_fusion.5 = (bf16[16,128,1024]{2,1,0:T(8,128)(2,1)}, bf16[16,128,1024]{2,1,0:T(8,128)(2,1)}) fusion(f32[16,1024]{1,0:T(8,128)S(1)} %get-tuple-element.909, f32[128,1024]{1,0:T(8,128)S(1)} %get-tuple-element.910, f32[16,1024]{1,0:T(8,128)S(1)} %get-tuple-element.911, f32[128,1024]{1,0:T(8,128)S(1)} %get-tuple-element.912), kind=kLoop, calls=%fused_computation.57.clone.1 | loop fusion | flops 16777216 | bytes 9568256 | tf_op jit(solution)/shard_map/convert.4
  331.7 4.5 %fusion.84 = f32[1,128,2048]{2,1,0:T(8,128)S(1)} fusion(bf16[16,128,1024]{2,1,0:T(8,128)(2,1)} %get-tuple-element.913, bf16[16,128,1024]{2,1,0:T(8,128)(2,1)} %get-tuple-element.914, f32[1,128,2048]{2,1,0:T(8,128)S(1)} %get-tuple-element.1005, f32[16,128,128]{2,1,0:T(8,128)S(1)} %bitcast.140, f32[128]{0:T(128)S(1)} %get-tuple-element.915, ...), kind=kOutput, calls=%fused_computation.60.clone.1 | convolution fusion | flops 1091567616 | bytes 11535360 | tf_op jit(solution)/shard_map/while/body/dot_general | solution.py:134
  345.6 4.8 %subtract_convert_fusion.5 = (bf16[16,128,1024]{2,1,0:T(8,128)(2,1)}, bf16[16,128,1024]{2,1,0:T(8,128)(2,1)}) fusion(f32[16,1024]{1,0:T(8,128)S(1)} %get-tuple-element.909, f32[128,1024]{1,0:T(8,128)S(1)} %get-tuple-element.910, f32[16,1024]{1,0:T(8,128)S(1)} %get-tuple-element.911, f32[128,1024]{1,0:T(8,128)S(1)} %get-tuple-element.912), kind=kLoop, calls=%fused_computation.57.clone.1 | loop fusion | flops 16777216 | bytes 9568256 | tf_op jit(solution)/shard_map/convert.4
  352.0 4.6 %fusion.84 = f32[1,128,2048]{2,1,0:T(8,128)S(1)} fusion(bf16[16,128,1024]{2,1,0:T(8,128)(2,1)} %get-tuple-element.913, bf16[16,128,1024]{2,1,0:T(8,128)(2,1)} %get-tuple-element.914, f32[1,128,2048]{2,1,0:T(8,128)S(1)} %get-tuple-element.1005, f32[16,128,128]{2,1,0:T(8,128)S(1)} %bitcast.140, f32[128]{0:T(128)S(1)} %get-tuple-element.915, ...), kind=kOutput, calls=%fused_computation.60.clone.1 | convolution fusion | flops 1091567616 | bytes 11535360 | tf_op jit(solution)/shard_map/while/body/dot_general | solution.py:134
  365.9 4.8 %subtract_convert_fusion.5 = (bf16[16,128,1024]{2,1,0:T(8,128)(2,1)}, bf16[16,128,1024]{2,1,0:T(8,128)(2,1)}) fusion(f32[16,1024]{1,0:T(8,128)S(1)} %get-tuple-element.909, f32[128,1024]{1,0:T(8,128)S(1)} %get-tuple-element.910, f32[16,1024]{1,0:T(8,128)S(1)} %get-tuple-element.911, f32[128,1024]{1,0:T(8,128)S(1)} %get-tuple-element.912), kind=kLoop, calls=%fused_computation.57.clone.1 | loop fusion | flops 16777216 | bytes 9568256 | tf_op jit(solution)/shard_map/convert.4
  372.3 4.5 %fusion.84 = f32[1,128,2048]{2,1,0:T(8,128)S(1)} fusion(bf16[16,128,1024]{2,1,0:T(8,128)(2,1)} %get-tuple-element.913, bf16[16,128,1024]{2,1,0:T(8,128)(2,1)} %get-tuple-element.914, f32[1,128,2048]{2,1,0:T(8,128)S(1)} %get-tuple-element.1005, f32[16,128,128]{2,1,0:T(8,128)S(1)} %bitcast.140, f32[128]{0:T(128)S(1)} %get-tuple-element.915, ...), kind=kOutput, calls=%fused_computation.60.clone.1 | convolution fusion | flops 1091567616 | bytes 11535360 | tf_op jit(solution)/shard_map/while/body/dot_general | solution.py:134
  386.2 4.8 %subtract_convert_fusion.5 = (bf16[16,128,1024]{2,1,0:T(8,128)(2,1)}, bf16[16,128,1024]{2,1,0:T(8,128)(2,1)}) fusion(f32[16,1024]{1,0:T(8,128)S(1)} %get-tuple-element.909, f32[128,1024]{1,0:T(8,128)S(1)} %get-tuple-element.910, f32[16,1024]{1,0:T(8,128)S(1)} %get-tuple-element.911, f32[128,1024]{1,0:T(8,128)S(1)} %get-tuple-element.912), kind=kLoop, calls=%fused_computation.57.clone.1 | loop fusion | flops 16777216 | bytes 9568256 | tf_op jit(solution)/shard_map/convert.4
  392.6 4.5 %fusion.84 = f32[1,128,2048]{2,1,0:T(8,128)S(1)} fusion(bf16[16,128,1024]{2,1,0:T(8,128)(2,1)} %get-tuple-element.913, bf16[16,128,1024]{2,1,0:T(8,128)(2,1)} %get-tuple-element.914, f32[1,128,2048]{2,1,0:T(8,128)S(1)} %get-tuple-element.1005, f32[16,128,128]{2,1,0:T(8,128)S(1)} %bitcast.140, f32[128]{0:T(128)S(1)} %get-tuple-element.915, ...), kind=kOutput, calls=%fused_computation.60.clone.1 | convolution fusion | flops 1091567616 | bytes 11535360 | tf_op jit(solution)/shard_map/while/body/dot_general | solution.py:134
  (223 shorter events, 79.2 us)
Async XLA Ops:
  0.6 9.5 %copy-start.2 = (s32[16]{0:T(128)S(1)}, s32[16]{0:T(128)}, u32[]{:S(2)}) copy-start(s32[16]{0:T(128)} %param.14) | copy-start | bytes 196
  0.6 10.1 %copy-start.1 = (bf16[128,2048]{1,0:T(8,128)(2,1)S(1)}, bf16[128,2048]{1,0:T(8,128)(2,1)}, u32[]{:S(2)}) copy-start(bf16[128,2048]{1,0:T(8,128)(2,1)} %param.12) | copy-start | bytes 1572868
  4.2 97.2 %all-to-all-start = ((bf16[16,64,2048]{2,1,0:T(8,128)(2,1)}), bf16[16,64,2048]{2,1,0:T(8,128)(2,1)}, u32[]{:S(2)}, u32[]{:S(2)}) async-start(bf16[16,64,2048]{2,1,0:T(8,128)(2,1)} %stack.2), calls=%async_computation | async-start | bytes 8388608 | tf_op jit(solution)/shard_map/all_to_all | solution.py:79
  398.6 1.0 copy-start
  398.6 1.0 copy-start.3
